TPU v7x, 32 devices: a whole 2x2x4 slice. The times are simulated.
32 devices in a mesh: groups: 2 (over x), seq: 16 (over z, y, core).
Axes of the slice: x: 2, y: 2, z: 4, core: 2. Of those that a mesh axis runs over, the one named last changes fastest.
Arguments:
- queries: bfloat16 [4096, 8192], P(('groups', 'seq')), parts along dimension 0, may hold values from -4.5 to 4.5
- keyvalue: bfloat16 [4096, 2048], P(('groups', 'seq')), parts along dimension 0, may hold values from -4.5 to 4.5
- doc_ids: int32 [4096], P(('groups', 'seq')), parts along dimension 0, may hold values from 0 to 7, never falling along the last dimension, each value on 1 to 512 neighbouring positions
- owner_tiles: int32 [32, 2], P(('groups', 'seq')), parts along dimension 0, may hold values from 0 to 15, as said below
- tile_counts: int32 [32], P(('groups', 'seq')), parts along dimension 0, may hold values from 0 to 2, as said below
Outputs:
- owned: bfloat16 [8192, 8192], P(('groups', 'seq')), parts along dimension 0
There are 2 independent parts, one for each index of `groups`. A program takes and returns all parts, laid end to end along the dimension named above; each array names one. Nothing has to cross between parts.
Inputs may be any that keep to these rules, and one draw needn't show every extreme that they name: `owner_tiles`: over the slots below each owner's count, every tile 0 to 15 is listed exactly once; the other slots hold 0. Tile t is listed either by its holder, the owner o with o * 128 <= t * 128 < (o + 1) * 128, or by the holder's partner, the owner whose index differs from the holder's by half the number of owners. `tile_counts`: the counts sum to 16; each is 0, 1 or 2, some owner has 2, and an owner has 2 exactly when its partner has 0.
All inputs are finite; a program needn't handle non-finite values.
Results may differ from a plain program's by a relative error of at most 0.0034.
Values may be sent and summed in bfloat16 or wider, within the bound.
A program may use at most 64 MiB of HBM per device.

v0:
```python
import functools
import math

import jax
import jax.numpy as jnp
from jax import lax
from jax.experimental import pallas as pl
from jax.experimental.pallas import tpu as pltpu
from jax.sharding import PartitionSpec as P

QUERY_HEADS = 64
KEY_VALUE_HEADS = 8
HEAD_WIDTH = 128
TILE = 128
DOCUMENT_LIMIT = 512

MESH = pl.DeviceIdType.MESH
NEAR_TILES = DOCUMENT_LIMIT // TILE + 1
BACK = NEAR_TILES - 1
GROUP_HEADS = QUERY_HEADS // KEY_VALUE_HEADS
HALF_HEADS = GROUP_HEADS // 2
HALF_COLS = HALF_HEADS * HEAD_WIDTH
PART_COLS = HALF_COLS // 2
GROUP_COLS = 2 * HALF_COLS
KV_COLS = 2 * HEAD_WIDTH
MASKED = -1e30
ROUNDS = 2
RAISE = HEAD_WIDTH ** -0.5 * math.log2(math.e)
VMEM = pl.BlockSpec(memory_space=pltpu.VMEM)
SMEM = pl.BlockSpec(memory_space=pltpu.SMEM)
HBM = pl.BlockSpec(memory_space=pltpu.HBM)
DMA = pltpu.SemaphoreType.DMA


class Place:
    def __init__(self, groups, count):
        self.me = me = lax.axis_index("seq")
        self.group = group = lax.axis_index("groups")
        self.core = lax.rem(me, 2)
        self.chip = chip = lax.div(me, 2)
        self.line = lax.rem(chip, 2)
        self.depth = lax.div(chip, 2)
        self.depths = count // 4
        self.reach = reach = self.depths // 2
        self.low = low = self.depth < reach
        step = jnp.where(low, 4, -4)
        self.inner = me + step
        self.outer = me - step
        self.rim = jnp.where(low, self.depth, self.depths - 1 - self.depth)
        self.crossing = self.rim == reach - 1
        self.sibling = me + 1 - 2 * self.core
        self.partner = lax.rem(me + count // 2, count)
        across = group + 1 - 2 * lax.rem(group, 2)
        beside = me + 2 - 4 * self.line
        self.giving = (jnp.where(low, across, group), jnp.where(low, me, beside))
        self.taking = (jnp.where(low, group, across), jnp.where(low, beside, me))


def remote(src, dst, send_sem, recv_sem, seq, group=None):
    to = {"seq": seq} if group is None else {"groups": group, "seq": seq}
    return pltpu.make_async_remote_copy(
        src_ref=src, dst_ref=dst, send_sem=send_sem, recv_sem=recv_sem,
        device_id=to, device_id_type=MESH)


class Flow:
    def __init__(self, at, rounds, o, sib, plan, far, farn, fars, farns, exo, exi, inj, injin, sends, recvs, turn):
        self.__dict__.update(locals())

    def trade(self, r, h):
        group, seq = self.at.giving
        return remote(self.exo.at[r, h], self.exi.at[r, h],
                      self.sends.at[0, r, h], self.recvs.at[0, r, h], seq, group)

    def inward(self, r, h):
        return remote(self.inj.at[r, h], self.injin.at[r, h],
                      self.sends.at[1, r, h], self.recvs.at[1, r, h], self.at.inner)

    def across(self, r, h):
        return remote(self.inj.at[r, h], self.far.at[r, h],
                      self.sends.at[1, r, h], self.recvs.at[2, r, h], self.at.inner)

    def outward(self, r, h):
        return remote(self.far.at[r, h], self.far.at[r, h],
                      self.sends.at[2, r, h], self.recvs.at[2, r, h], self.at.outer)

    def deliver(self, r, h):
        group, seq = self.at.taking
        return remote(self.far.at[r, h], self.farn.at[r, h],
                      self.sends.at[3, r, h], self.recvs.at[3, r, h], seq, group)

    def hand(self, r, h):
        return remote(self.far.at[r, h], self.fars.at[r, h],
                      self.sends.at[4, r, h], self.recvs.at[4, r, h], self.at.sibling)

    def handn(self, r, h):
        return remote(self.farn.at[r, h], self.farns.at[r, h],
                      self.sends.at[5, r, h], self.recvs.at[5, r, h], self.at.sibling)

    def here(self, row, r):
        return jnp.broadcast_to(self.plan[8 * row:8 * row + 1, :] == self.turn(r), (TILE, TILE))

    def offer(self, h):
        for r in range(self.rounds):
            own_here = self.here(0, r)
            for c in range(0, PART_COLS, TILE):
                cols, there = slice(c, c + TILE), slice(PART_COLS + c, PART_COLS + c + TILE)
                own = self.o[h, self.at.core, :, there].astype(jnp.float32)
                sib = self.sib[h, :, there].astype(jnp.float32)
                self.exo[r, h, :, cols] = jnp.where(own_here, own, sib).astype(jnp.bfloat16)
            self.trade(r, h).start()

    def compose(self, r, h, below):
        own_here, sib_here = self.here(0, r), self.here(1, r)
        nbr_here = self.here(2, r) | self.here(3, r)
        for c in range(0, PART_COLS, TILE):
            cols = slice(c, c + TILE)
            new = self.exi[r, h, :, cols].astype(jnp.float32)
            if below:
                new = jnp.where(nbr_here, new, self.injin[r, h, :, cols].astype(jnp.float32))
            new = jnp.where(sib_here, self.sib[h, :, cols].astype(jnp.float32), new)
            own = self.o[h, self.at.core, :, cols].astype(jnp.float32)
            self.inj[r, h, :, cols] = jnp.where(own_here, own, new).astype(jnp.bfloat16)

    def inject(self, h):
        for r in range(self.rounds):
            self.trade(r, h).wait_recv()

            @pl.when(self.at.rim == 0)
            def _():
                self.compose(r, h, False)

            @pl.when(self.at.rim > 0)
            def _():
                self.inward(r, h).wait_recv()
                self.compose(r, h, True)

            @pl.when(self.at.crossing)
            def _():
                self.across(r, h).start()

            @pl.when(jnp.logical_not(self.at.crossing))
            def _():
                self.inward(r, h).start()

    def forward(self, h):
        for r in range(self.rounds):
            self.outward(r, h).wait_recv()

            @pl.when(self.at.rim > 0)
            def _():
                self.outward(r, h).start()

            self.deliver(r, h).start()
            self.hand(r, h).start()

    def finish(self, h):
        for r in range(self.rounds):
            self.deliver(r, h).wait_recv()
            self.handn(r, h).start()

    def stages(self, first):
        at = self.at
        arrive = first + 1 + at.reach + at.reach - 1 - at.rim
        return ((first, self.offer), (first + 1 + at.rim, self.inject),
                (arrive, self.forward), (arrive + 1, self.finish))

    def steps(self, first):
        return KEY_VALUE_HEADS + first + 1 + 2 * self.at.reach

    def drain(self, h):
        for r in range(self.rounds):
            self.trade(r, h).wait_send()
            self.inward(r, h).wait_send()

            @pl.when(self.at.rim > 0)
            def _():
                self.outward(r, h).wait_send()

            self.deliver(r, h).wait_send()
            self.hand(r, h).wait()
            self.handn(r, h).wait()


def each(n, body):
    lax.fori_loop(0, n, lambda i, c: (body(i), c)[1], 0)


heads = functools.partial(each, KEY_VALUE_HEADS)


def run_stages(steps, stages):
    def step(u):
        for lag, stage in stages:
            h = u - lag

            @pl.when((h >= 0) & (h < KEY_VALUE_HEADS))
            def _():
                stage(h)

    each(steps, step)


def main_kernel(groups, count, kv_hbm, q_hbm, docs, counts,
                o, sib, far, farn, fars, farns, plan,
                q, kv, mark, marks, given, gathered, bias, vals, exo, exi, inj, injin,
                ql, kvl, share_s, share_r, mark_s, mark_r, given_s, given_r, info_s, info_r,
                kv_s, kv_r, flow_s, flow_r):
    at = Place(groups, count)
    me, core, chip, line, group = at.me, at.core, at.chip, at.line, at.group
    chips = count // 2
    flow = Flow(at, ROUNDS, o, sib, plan, far, farn, fars, farns, exo, exi, inj, injin,
                flow_s, flow_r, lambda r: r)

    def own(h):
        return kv_hbm.at[:, pl.ds(pl.multiple_of(h * KV_COLS, KV_COLS), KV_COLS)]

    def local(h):
        return pltpu.make_async_copy(own(h), kv.at[h, 4 + core], kvl.at[h])

    def q_copy(h):
        cols = pl.ds(pl.multiple_of(h * GROUP_COLS, GROUP_COLS), GROUP_COLS)
        return pltpu.make_async_copy(q_hbm.at[:, cols], q.at[:, cols], ql.at[h])

    def share(h):
        return remote(o.at[h, 1 - core], sib.at[h], share_s.at[h], share_r.at[h], at.sibling)

    def up_two(h):
        return remote(own(h), kv.at[h, core], kv_s.at[0, h], kv_r.at[h, core], me + 4)

    def up_one(h):
        return remote(own(h), kv.at[h, 2 + core], kv_s.at[1, h], kv_r.at[h, 2 + core], me + 2)

    def relay_one(h):
        return remote(kv.at[h, core], kv.at[h, 2 + core], kv_s.at[1, h], kv_r.at[h, 2 + core], me - 2)

    def sib_own(h):
        return remote(own(h), kv.at[h, 4], kv_s.at[2, h], kv_r.at[h, 4], at.sibling)

    def sib_one(h):
        return remote(kv.at[h, 2 + core], kv.at[h, 2 + core], kv_s.at[3, h],
                      kv_r.at[h, 2 + core], at.sibling)

    def sib_two(h):
        return remote(kv.at[h, 1], kv.at[h, 1], kv_s.at[4, h], kv_r.at[h, 1], at.sibling)

    def arrived(h, slot):
        remote(kv.at[h, slot], kv.at[h, slot], kv_s.at[0, h], kv_r.at[h, slot],
               at.sibling).wait_recv()

    def mark_to(k):
        return remote(mark, marks.at[BACK - k], mark_s.at[BACK - k], mark_r.at[BACK - k], me + k)

    def given_to(by):
        return remote(given.at[group], given.at[group], given_s.at[by], given_r.at[group],
                      me, lax.rem(group + by, groups))

    def given_from(by):
        other = lax.rem(group + by, groups)
        return remote(given.at[other], given.at[other], given_s.at[by], given_r.at[other], me, other)

    def info_to(peer):
        return remote(given, gathered.at[me], info_s.at[peer], info_r.at[me], peer)

    def info_from(peer):
        return remote(given, gathered.at[peer], info_s.at[peer], info_r.at[peer], peer)

    def peers(body):
        def one(i):
            body(lax.rem(me + 1 + i, count))
        each(count - 1, one)

    heads(lambda h: local(h).start())
    heads(lambda h: q_copy(h).start())
    mark[...] = jnp.broadcast_to(docs[...], (8, TILE))
    given[group] = jnp.full((8, TILE), counts[0], jnp.int32)

    barrier = pltpu.get_barrier_semaphore()
    peers(lambda p: pl.semaphore_signal(barrier, inc=1, device_id={"seq": p}, device_id_type=MESH))
    for by in range(1, groups):
        pl.semaphore_signal(barrier, inc=1, device_id={"groups": lax.rem(group + by, groups)},
                            device_id_type=MESH)
    pl.semaphore_wait(barrier, count - 1 + groups - 1)

    has_two_up = chip + 2 < chips

    def launch(h):
        @pl.when(has_two_up)
        def _():
            up_two(h).start()

        @pl.when(line == 0)
        def _():
            up_one(h).start()

        @pl.when(core == 0)
        def _():
            sib_own(h).start()

    launch(0)
    for by in range(1, groups):
        given_to(by).start()
    for k in range(1, NEAR_TILES):
        @pl.when(me + k < count)
        def _():
            mark_to(k).start()
    each(KEY_VALUE_HEADS - 1, lambda h: launch(h + 1))

    blank = jnp.zeros((TILE, KV_COLS), jnp.bfloat16)

    @pl.when(chip < 2)
    def _():
        def clear(h):
            kv[h, 0] = blank
            kv[h, 1] = blank
        heads(clear)

    @pl.when(chip < 1)
    def _():
        def clear(h):
            kv[h, 2] = blank
            kv[h, 3] = blank
        heads(clear)

    vals[:, HEAD_WIDTH:] = jnp.ones((NEAR_TILES * TILE, HEAD_WIDTH), jnp.bfloat16)

    for by in range(1, groups):
        given_from(by).wait_recv()
    peers(lambda p: info_to(p).start())
    gathered[me] = given[...]

    rows = lax.broadcasted_iota(jnp.int32, (TILE, TILE), 0)
    cols = lax.broadcasted_iota(jnp.int32, (TILE, TILE), 1)
    mine = jnp.broadcast_to(mark[0:1, :], (TILE, TILE))
    asked = mine.T
    bias[:, BACK * TILE:] = jnp.where((asked == mine) & (cols <= rows), 0.0, MASKED).astype(jnp.float32)
    for w in range(BACK):
        past = slice(w * TILE, (w + 1) * TILE)

        @pl.when(me - BACK + w < 0)
        def _():
            bias[:, past] = jnp.full((TILE, TILE), MASKED, jnp.float32)

        @pl.when(me - BACK + w >= 0)
        def _():
            mark_to(BACK - w).wait_recv()
            allowed = asked == jnp.broadcast_to(marks[w, 0:1, :], (TILE, TILE))
            bias[:, past] = jnp.where(allowed, 0.0, MASKED).astype(jnp.float32)

    def tally():
        peers(lambda p: info_from(p).wait_recv())
        half = count // 2
        other_group, other = at.giving
        other_sib = other + 1 - 2 * core
        targets = ((group, me), (group, at.sibling), (other_group, other), (other_group, other_sib),
                   (group, at.partner))

        def bin_of(g, i):
            up = i < half
            return jnp.where(up, 2 * lax.div(g, 2) + lax.rem(lax.div(i, 2), 2), groups + g)

        wanted = [(bin_of(g, i), g * count + i) for g, i in targets]

        def add(i, carry):
            ahead, totals = carry
            for g in range(groups):
                gives = jnp.where(gathered[i, g] == 0, 1, 0)
                here, order = bin_of(g, i), g * count + i
                ahead = tuple(
                    a + gives * jnp.where((here == b) & (order < n), 1, 0)
                    for a, (b, n) in zip(ahead, wanted))
                totals = tuple(t + gives * jnp.where(here == b, 1, 0) for b, t in enumerate(totals))
            return ahead, totals

        zero = jnp.zeros((8, TILE), jnp.int32)
        ahead, totals = lax.fori_loop(
            0, count, add, ((zero,) * len(targets), (zero,) * (2 * groups)))
        for slot, ((g, i), a) in enumerate(zip(targets, ahead)):
            gives = gathered[i, g] == 0
            plan[8 * slot:8 * slot + 8, :] = jnp.where(gives, a, -1)
        most = totals[0]
        for t in totals[1:]:
            most = jnp.maximum(most, t)
        plan[8 * len(targets):8 * len(targets) + 8, :] = most

    def attend(h):
        vals[:, 0:HEAD_WIDTH] = kv[h, pl.ds(core, NEAR_TILES), :, HEAD_WIDTH:].reshape(
            NEAR_TILES * TILE, HEAD_WIDTH)
        keys = kv[h, pl.ds(core, NEAR_TILES), :, 0:HEAD_WIDTH].reshape(NEAR_TILES * TILE, HEAD_WIDTH)
        summed = vals[...]
        for j in range(GROUP_HEADS):
            at_col = pl.multiple_of((h * GROUP_HEADS + j) * HEAD_WIDTH, HEAD_WIDTH)
            s = lax.dot_general(q[:, pl.ds(at_col, HEAD_WIDTH)], keys, (((1,), (1,)), ((), ())),
                                preferred_element_type=jnp.float32) + bias[...]
            e = jnp.exp2((s - jnp.max(s, axis=1, keepdims=True)) * RAISE)
            mixed = jnp.dot(e.astype(jnp.bfloat16), summed, preferred_element_type=jnp.float32)
            c = (j % HALF_HEADS) * HEAD_WIDTH
            o[h, j // HALF_HEADS, :, c:c + HEAD_WIDTH] = (
                mixed[:, 0:HEAD_WIDTH] / mixed[:, HEAD_WIDTH:]).astype(jnp.bfloat16)

    def relay_two(h):
        @pl.when(chip >= 2)
        def _():
            arrived(h, core)

            @pl.when(line == 1)
            def _():
                relay_one(h).start()

            @pl.when(core == 1)
            def _():
                sib_two(h).start()

    def relay_sib(h):
        @pl.when(chip >= 1)
        def _():
            arrived(h, 2 + core)
            sib_one(h).start()

    def compute(h):
        @pl.when(chip >= 1)
        def _():
            arrived(h, 3 - core)

        @pl.when((chip >= 2) & (core == 0))
        def _():
            arrived(h, 1)

        @pl.when(core == 1)
        def _():
            arrived(h, 4)

        local(h).wait()
        q_copy(h).wait()
        attend(h)
        share(h).start()

    def shared(h):
        @pl.when(h == 0)
        def _():
            tally()

        share(h).wait_recv()

    stages = ((0, relay_two), (1, relay_sib), (2, compute), (3, shared)) + flow.stages(3)
    run_stages(flow.steps(3), stages)

    def drain(h):
        flow.drain(h)
        share(h).wait_send()

        @pl.when(has_two_up)
        def _():
            up_two(h).wait_send()

        @pl.when((line == 0) | (chip >= 2))
        def _():
            up_one(h).wait_send()

        @pl.when(core == 0)
        def _():
            sib_own(h).wait_send()

        @pl.when(chip >= 1)
        def _():
            sib_one(h).wait_send()

        @pl.when((chip >= 2) & (core == 1))
        def _():
            sib_two(h).wait_send()

    heads(drain)
    peers(lambda p: info_to(p).wait_send())
    for by in range(1, groups):
        given_to(by).wait_send()
    for k in range(1, NEAR_TILES):
        @pl.when(me + k < count)
        def _():
            mark_to(k).wait_send()


def round_kernel(groups, count, o, sib, plan, turn, far, farn, fars, farns,
                 exo, exi, inj, injin, flow_s, flow_r):
    at = Place(groups, count)
    barrier = pltpu.get_barrier_semaphore()

    def greet(seq, group=at.group):
        pl.semaphore_signal(barrier, inc=1, device_id={"groups": group, "seq": seq}, device_id_type=MESH)

    greet(at.sibling)
    greet(at.inner)
    greet(at.giving[1], at.giving[0])
    greet(at.taking[1], at.taking[0])

    @pl.when(at.rim > 0)
    def _():
        greet(at.outer)

    pl.semaphore_wait(barrier, jnp.where(at.rim > 0, 5, 4))

    flow = Flow(at, 1, o, sib, plan, far, farn, fars, farns, exo, exi, inj, injin,
                flow_s, flow_r, lambda r: turn[0:1, :])
    run_stages(flow.steps(0), flow.stages(0))
    heads(flow.drain)


def place_kernel(extra, tiles, valid, plan, o, *rest):
    fars, out, blank, sems = rest[:-3], rest[-3], rest[-2], rest[-1]
    me = lax.axis_index("seq")
    core = lax.rem(me, 2)
    slots = out.shape[0] // TILE
    blank[...] = jnp.zeros_like(blank)
    rank = plan[4 * 8, 0]
    main, late = fars[:4], fars[4:]
    turn = jnp.clip(rank, 0, ROUNDS - 1)

    def spot(h, lane, part):
        at = (2 * h + lane) * HALF_COLS + part * PART_COLS
        return pl.ds(pl.multiple_of(at, PART_COLS), PART_COLS)

    def parts(h):
        mine = [(o.at[h, lane, :, pl.ds(part * PART_COLS, PART_COLS)], spot(h, lane, part))
                for lane in (0, 1) for part in (0, 1)]
        where = [spot(h, lane, part) for lane in (core, 1 - core) for part in (0, 1)]
        theirs = [(ref.at[turn, h], cols) for ref, cols in zip(main, where)]
        later = [(ref.at[0, h], cols) for ref, cols in zip(late, where)]
        none = [(blank, cols) for _, cols in mine]
        return mine, theirs, later, none

    def run(h, c, go):
        for s in range(slots):
            live = s < valid[0]
            own = live & (tiles[0, s] == me)
            moved = live & jnp.logical_not(own)
            soon = moved & (rank < ROUNDS) if extra else moved
            cases = (own, soon, moved & (rank >= ROUNDS), jnp.logical_not(live))
            for case, pieces in zip(cases, parts(h)):
                if not pieces:
                    continue

                @pl.when(case)
                def _():
                    for k, (src, cols) in enumerate(pieces):
                        go(pltpu.make_async_copy(
                            src, out.at[pl.ds(s * TILE, TILE), cols], sems.at[h, s, k]))
        return c

    lax.fori_loop(0, KEY_VALUE_HEADS, functools.partial(run, go=lambda x: x.start()), 0)
    lax.fori_loop(0, KEY_VALUE_HEADS, functools.partial(run, go=lambda x: x.wait()), 0)


def local(groups, count, queries, keyvalue, doc_ids, owner_tiles, tile_counts):
    width = queries.shape[1]
    slots = owner_tiles.shape[1]
    H = KEY_VALUE_HEADS
    bf, i32 = jnp.bfloat16, jnp.int32
    half = (H, TILE, HALF_COLS)

    def part(rounds):
        return (rounds, H, TILE, PART_COLS)

    *held, plan = pl.pallas_call(
        functools.partial(main_kernel, groups, count),
        out_shape=[
            jax.ShapeDtypeStruct((H, 2, TILE, HALF_COLS), bf),
            jax.ShapeDtypeStruct(half, bf),
        ] + [jax.ShapeDtypeStruct(part(ROUNDS), bf)] * 4 + [
            jax.ShapeDtypeStruct((48, TILE), i32),
        ],
        in_specs=[HBM, HBM, VMEM, SMEM],
        out_specs=[VMEM] * 7,
        scratch_shapes=[
            pltpu.VMEM(queries.shape, bf),
            pltpu.VMEM((H, 6, TILE, KV_COLS), bf),
            pltpu.VMEM((8, TILE), i32),
            pltpu.VMEM((BACK, 8, TILE), i32),
            pltpu.VMEM((groups, 8, TILE), i32),
            pltpu.VMEM((count, groups, 8, TILE), i32),
            pltpu.VMEM((TILE, NEAR_TILES * TILE), jnp.float32),
            pltpu.VMEM((NEAR_TILES * TILE, 2 * HEAD_WIDTH), bf),
        ] + [pltpu.VMEM(part(ROUNDS), bf)] * 4 + [
            DMA((H,)),
            DMA((H,)),
            DMA((H,)),
            DMA((H,)),
            DMA((BACK,)),
            DMA((BACK,)),
            DMA((groups,)),
            DMA((groups,)),
            DMA((count,)),
            DMA((count,)),
            DMA((5, H)),
            DMA((H, 6)),
            DMA((6, ROUNDS, H)),
            DMA((6, ROUNDS, H)),
        ],
        compiler_params=pltpu.CompilerParams(
            collective_id=0, has_side_effects=True, vmem_limit_bytes=40 << 20),
    )(keyvalue, queries, doc_ids[None, :], tile_counts)
    o, sib, *far = held

    def again(turn):
        turns = jnp.full((8, TILE), turn, i32)
        return pl.pallas_call(
            functools.partial(round_kernel, groups, count),
            out_shape=[jax.ShapeDtypeStruct(part(1), bf)] * 4,
            in_specs=[VMEM] * 4,
            out_specs=[VMEM] * 4,
            scratch_shapes=[pltpu.VMEM(part(1), bf)] * 4 + [DMA((6, 1, H)), DMA((6, 1, H))],
            compiler_params=pltpu.CompilerParams(
                collective_id=1, has_side_effects=True, vmem_limit_bytes=24 << 20),
        )(o, sib, plan, turns)

    def place(late):
        return pl.pallas_call(
            functools.partial(place_kernel, bool(late)),
            out_shape=jax.ShapeDtypeStruct((slots * TILE, width), bf),
            in_specs=[SMEM] * 3 + [VMEM] * (5 + len(late)),
            out_specs=pl.BlockSpec(memory_space=pl.ANY),
            scratch_shapes=[pltpu.VMEM((TILE, PART_COLS), bf), DMA((H, slots, 4))],
            compiler_params=pltpu.CompilerParams(vmem_limit_bytes=16 << 20),
        )(owner_tiles, tile_counts, plan, o, *far, *late)

    most = plan[40, 0]

    def more():
        def one(turn, kept):
            here = plan[32, 0] == turn
            return tuple(jnp.where(here, n, k) for n, k in zip(again(turn), kept))

        return place(lax.fori_loop(ROUNDS, most, one, tuple(jnp.zeros(part(1), bf) for _ in range(4))))

    return lax.cond(most > ROUNDS, more, lambda: place(()))


def solution(mesh):
    spread = P(("groups", "seq"))
    rows = P(("groups", "seq"), None)
    return jax.shard_map(
        functools.partial(local, mesh.shape["groups"], mesh.shape["seq"]), mesh=mesh,
        in_specs=(rows, rows, spread, rows, spread), out_specs=rows, check_vma=False)
```

profile of v0, /device:TPU:0, one launch (start us, length us, event | category | flops | bytes accessed | tf_op | source)
XLA Modules:
  0.0 87.5 jit_solution(9497104292566009741)
XLA Ops:
  0.7 0.0 copy-start
  0.7 1.6 %copy-done = bf16[128,8192]{1,0:T(8,128)(2,1)S(1)} copy-done((bf16[128,8192]{1,0:T(8,128)(2,1)S(1)}, bf16[128,8192]{1,0:T(8,128)(2,1)}, u32[]{:S(2)}) %copy-start) | copy-done | bytes 2097176
  2.2 0.0 copy-start.1
  2.2 1.0 %copy-done.1 = bf16[128,2048]{1,0:T(8,128)(2,1)S(1)} copy-done((bf16[128,2048]{1,0:T(8,128)(2,1)S(1)}, bf16[128,2048]{1,0:T(8,128)(2,1)}, u32[]{:S(2)}) %copy-start.1) | copy-done | bytes 524312
  3.3 0.0 copy-start.2
  3.3 0.7 copy-done.2
  3.9 75.9 %shard_map.57 = (bf16[8,2,128,512]{3,2,1,0:T(8,128)(2,1)S(1)}, bf16[8,128,512]{2,1,0:T(8,128)(2,1)S(1)}, bf16[2,8,128,256]{3,2,1,0:T(8,128)(2,1)}, bf16[2,8,128,...) custom-call(bf16[128,2048]{1,0:T(8,128)(2,1)S(1)} %copy-done.1, ...), custom_call_target="tpu_custom_call" | custom-call | tf_op jit(solution)/shard_map/pallas_call | solution.py:562
  79.8 0.5 slice.6
  81.0 4.5 %conditional.1 = (bf16[256,8192]{1,0:T(8,128)(2,1)S(1)}) conditional(s32[]{:T(128)} %convert_element_type.3, (s32[1,2]{1,0:T(1,128)}, s32[1]{0:T(128)}, s32[48,128]{1,0:T(8,128)S(1)}, bf16[8,2,128,512]{3,2,1,0:T(8,128)(2,1)S(1)}, bf16[2,8,128,256]{3,2,1,0:T(8,128)(2,1)}, /*index=5*/bf16[2,8,128,256]{3,2,1,0:T(8,128)(2,1)}, ...), branch_computations={%region_0.0_spmd, %region_1.4_spmd} | conditional | flops 1048579 | bytes 16781720 | solution.py:633
  81.0 4.5 %branch_0_fun.1 = bf16[256,8192]{1,0:T(8,128)(2,1)S(1)} custom-call(s32[1,2]{1,0:T(1,128)} %get-tuple-element.80.tiles, s32[1]{0:T(128)} %get-tuple-element.81.valid, s32[48,128]{1,0:T(8,128)S(1)} %get-tuple-element.82.plan, bf16[8,2,128,512]{3,2,1,0:T(8,128)(2,1)S(1)} %get-tuple-element.83.o, bf16[2,8,128,256]{3,2,1,0:T(8,128)(2,1)} %get-tuple-element.84.rest_0_, ...), custom_call_target="tpu_custom_call" | custom-call | tf_op jit(solution)/shard_map/cond/branch_0_fun/pallas_call | solution.py:615
  85.5 0.0 copy-start.7
  85.5 2.0 %copy-done.7 = bf16[256,8192]{1,0:T(8,128)(2,1)} copy-done((bf16[256,8192]{1,0:T(8,128)(2,1)}, bf16[256,8192]{1,0:T(8,128)(2,1)S(1)}, u32[]{:S(2)}) %copy-start.7) | copy-done | bytes 4194328
Async XLA Ops:
  0.7 1.6 %copy-start = (bf16[128,8192]{1,0:T(8,128)(2,1)S(1)}, bf16[128,8192]{1,0:T(8,128)(2,1)}, u32[]{:S(2)}) copy-start(bf16[128,8192]{1,0:T(8,128)(2,1)} %q_hbm.1) | copy-start | bytes 6291460
  2.2 1.0 %copy-start.1 = (bf16[128,2048]{1,0:T(8,128)(2,1)S(1)}, bf16[128,2048]{1,0:T(8,128)(2,1)}, u32[]{:S(2)}) copy-start(bf16[128,2048]{1,0:T(8,128)(2,1)} %kv_hbm.1) | copy-start | bytes 1572868
  3.3 0.7 copy-start.2
  85.5 2.0 %copy-start.7 = (bf16[256,8192]{1,0:T(8,128)(2,1)}, bf16[256,8192]{1,0:T(8,128)(2,1)S(1)}, u32[]{:S(2)}) copy-start(bf16[256,8192]{1,0:T(8,128)(2,1)S(1)} %get-tuple-element.259) | copy-start | bytes 12582916
where the time goes:
time: 87.8 us; the launch traced here: 87.5 us
  Pallas kernels  80.4 us (92%)
  local copies, waits for them, and re-layouts  5.82 us (7%)
  between operations  1.33 us (2%)
    pallas_call x1, Pallas kernels, local(): pl.pallas_call(functools.partial(main_kernel, groups, count), out_shape=[...  75.9 us
    unnamed x8, local copies, waits for them, and re-layouts  5.29 us
    pallas_call x1, Pallas kernels, place(): pl.pallas_call(functools.partial(place_kernel, bool(late)), out_shape=jax...  4.49 us

commit v1 on v0

--- a/solution.py
+++ b/solution.py
@@ -24,7 +24,9 @@
 GROUP_COLS = 2 * HALF_COLS
 KV_COLS = 2 * HEAD_WIDTH
 MASKED = -1e30
-ROUNDS = 2
+SPLITS = 1
+HOP = 3
+FUSED = 4
 RAISE = HEAD_WIDTH ** -0.5 * math.log2(math.e)
 VMEM = pl.BlockSpec(memory_space=pltpu.VMEM)
 SMEM = pl.BlockSpec(memory_space=pltpu.SMEM)
@@ -64,122 +66,122 @@
 
 
 class Flow:
-    def __init__(self, at, rounds, o, sib, plan, far, farn, fars, farns, exo, exi, inj, injin, sends, recvs, turn):
+    def __init__(self, at, rounds, splits, o, sib, plan, far, farn, fars, farns, exo, exi, inj, injin,
+                 sends, recvs, turn):
         self.__dict__.update(locals())
-
-    def trade(self, r, h):
+        self.items = KEY_VALUE_HEADS * splits * rounds
+        self.rows = TILE // splits
+
+    def copy(self, kind, i, src, dst, seq, group=None, lands=None):
+        lands = kind if lands is None else lands
+        return remote(src.at[i], dst.at[i], self.sends.at[kind, i], self.recvs.at[lands, i], seq, group)
+
+    def trade(self, i):
         group, seq = self.at.giving
-        return remote(self.exo.at[r, h], self.exi.at[r, h],
-                      self.sends.at[0, r, h], self.recvs.at[0, r, h], seq, group)
-
-    def inward(self, r, h):
-        return remote(self.inj.at[r, h], self.injin.at[r, h],
-                      self.sends.at[1, r, h], self.recvs.at[1, r, h], self.at.inner)
-
-    def across(self, r, h):
-        return remote(self.inj.at[r, h], self.far.at[r, h],
-                      self.sends.at[1, r, h], self.recvs.at[2, r, h], self.at.inner)
-
-    def outward(self, r, h):
-        return remote(self.far.at[r, h], self.far.at[r, h],
-                      self.sends.at[2, r, h], self.recvs.at[2, r, h], self.at.outer)
-
-    def deliver(self, r, h):
+        return self.copy(0, i, self.exo, self.exi, seq, group)
+
+    def inward(self, i):
+        return self.copy(1, i, self.inj, self.injin, self.at.inner)
+
+    def across(self, i):
+        return self.copy(1, i, self.inj, self.far, self.at.inner, lands=2)
+
+    def outward(self, i):
+        return self.copy(2, i, self.far, self.far, self.at.outer)
+
+    def deliver(self, i):
         group, seq = self.at.taking
-        return remote(self.far.at[r, h], self.farn.at[r, h],
-                      self.sends.at[3, r, h], self.recvs.at[3, r, h], seq, group)
-
-    def hand(self, r, h):
-        return remote(self.far.at[r, h], self.fars.at[r, h],
-                      self.sends.at[4, r, h], self.recvs.at[4, r, h], self.at.sibling)
-
-    def handn(self, r, h):
-        return remote(self.farn.at[r, h], self.farns.at[r, h],
-                      self.sends.at[5, r, h], self.recvs.at[5, r, h], self.at.sibling)
-
-    def here(self, row, r):
-        return jnp.broadcast_to(self.plan[8 * row:8 * row + 1, :] == self.turn(r), (TILE, TILE))
-
-    def offer(self, h):
-        for r in range(self.rounds):
-            own_here = self.here(0, r)
-            for c in range(0, PART_COLS, TILE):
-                cols, there = slice(c, c + TILE), slice(PART_COLS + c, PART_COLS + c + TILE)
-                own = self.o[h, self.at.core, :, there].astype(jnp.float32)
-                sib = self.sib[h, :, there].astype(jnp.float32)
-                self.exo[r, h, :, cols] = jnp.where(own_here, own, sib).astype(jnp.bfloat16)
-            self.trade(r, h).start()
-
-    def compose(self, r, h, below):
-        own_here, sib_here = self.here(0, r), self.here(1, r)
-        nbr_here = self.here(2, r) | self.here(3, r)
+        return self.copy(3, i, self.far, self.farn, seq, group)
+
+    def hand(self, i):
+        return self.copy(4, i, self.far, self.fars, self.at.sibling)
+
+    def handn(self, i):
+        return self.copy(5, i, self.farn, self.farns, self.at.sibling)
+
+    def spot(self, i):
+        h = lax.div(i, self.splits * self.rounds)
+        p = lax.rem(lax.div(i, self.rounds), self.splits)
+        rows = pl.ds(pl.multiple_of(p * self.rows, self.rows), self.rows)
+        turn = self.turn(lax.rem(i, self.rounds))
+        heres = [jnp.broadcast_to(self.plan[8 * k:8 * k + 1, :] == turn, (self.rows, TILE)) for k in range(4)]
+        return h, rows, heres
+
+    def offer(self, i):
+        h, rows, (own_here, *_) = self.spot(i)
+        for c in range(0, PART_COLS, TILE):
+            cols, there = slice(c, c + TILE), slice(PART_COLS + c, PART_COLS + c + TILE)
+            own = self.o[h, self.at.core, rows, there].astype(jnp.float32)
+            sib = self.sib[h, rows, there].astype(jnp.float32)
+            self.exo[i, :, cols] = jnp.where(own_here, own, sib).astype(jnp.bfloat16)
+        self.trade(i).start()
+
+    def compose(self, i, below):
+        h, rows, (own_here, sib_here, near, far) = self.spot(i)
+        nbr_here = near | far
         for c in range(0, PART_COLS, TILE):
             cols = slice(c, c + TILE)
-            new = self.exi[r, h, :, cols].astype(jnp.float32)
+            new = self.exi[i, :, cols].astype(jnp.float32)
             if below:
-                new = jnp.where(nbr_here, new, self.injin[r, h, :, cols].astype(jnp.float32))
-            new = jnp.where(sib_here, self.sib[h, :, cols].astype(jnp.float32), new)
-            own = self.o[h, self.at.core, :, cols].astype(jnp.float32)
-            self.inj[r, h, :, cols] = jnp.where(own_here, own, new).astype(jnp.bfloat16)
-
-    def inject(self, h):
-        for r in range(self.rounds):
-            self.trade(r, h).wait_recv()
-
-            @pl.when(self.at.rim == 0)
-            def _():
-                self.compose(r, h, False)
-
-            @pl.when(self.at.rim > 0)
-            def _():
-                self.inward(r, h).wait_recv()
-                self.compose(r, h, True)
-
-            @pl.when(self.at.crossing)
-            def _():
-                self.across(r, h).start()
-
-            @pl.when(jnp.logical_not(self.at.crossing))
-            def _():
-                self.inward(r, h).start()
-
-    def forward(self, h):
-        for r in range(self.rounds):
-            self.outward(r, h).wait_recv()
-
-            @pl.when(self.at.rim > 0)
-            def _():
-                self.outward(r, h).start()
-
-            self.deliver(r, h).start()
-            self.hand(r, h).start()
-
-    def finish(self, h):
-        for r in range(self.rounds):
-            self.deliver(r, h).wait_recv()
-            self.handn(r, h).start()
-
-    def stages(self, first):
+                new = jnp.where(nbr_here, new, self.injin[i, :, cols].astype(jnp.float32))
+            new = jnp.where(sib_here, self.sib[h, rows, cols].astype(jnp.float32), new)
+            own = self.o[h, self.at.core, rows, cols].astype(jnp.float32)
+            self.inj[i, :, cols] = jnp.where(own_here, own, new).astype(jnp.bfloat16)
+
+    def inject(self, i):
+        self.trade(i).wait_recv()
+
+        @pl.when(self.at.rim == 0)
+        def _():
+            self.compose(i, False)
+
+        @pl.when(self.at.rim > 0)
+        def _():
+            self.inward(i).wait_recv()
+            self.compose(i, True)
+
+        @pl.when(self.at.crossing)
+        def _():
+            self.across(i).start()
+
+        @pl.when(jnp.logical_not(self.at.crossing))
+        def _():
+            self.inward(i).start()
+
+    def forward(self, i):
+        self.outward(i).wait_recv()
+
+        @pl.when(self.at.rim > 0)
+        def _():
+            self.outward(i).start()
+
+        self.deliver(i).start()
+        self.hand(i).start()
+
+    def finish(self, i):
+        self.deliver(i).wait_recv()
+        self.handn(i).start()
+
+    def stages(self, first, hop):
         at = self.at
-        arrive = first + 1 + at.reach + at.reach - 1 - at.rim
-        return ((first, self.offer), (first + 1 + at.rim, self.inject),
-                (arrive, self.forward), (arrive + 1, self.finish))
-
-    def steps(self, first):
-        return KEY_VALUE_HEADS + first + 1 + 2 * self.at.reach
-
-    def drain(self, h):
-        for r in range(self.rounds):
-            self.trade(r, h).wait_send()
-            self.inward(r, h).wait_send()
-
-            @pl.when(self.at.rim > 0)
-            def _():
-                self.outward(r, h).wait_send()
-
-            self.deliver(r, h).wait_send()
-            self.hand(r, h).wait()
-            self.handn(r, h).wait()
+        arrive = first + hop * (2 * at.reach - at.rim)
+        return ((arrive + hop, 1, self.items, self.finish), (arrive, 1, self.items, self.forward),
+                (first + hop * (1 + at.rim), 1, self.items, self.inject), (first, 1, self.items, self.offer))
+
+    def steps(self, first, hop):
+        return self.items + first + hop * (2 * self.at.reach + 1)
+
+    def drain(self, i):
+        self.trade(i).wait_send()
+        self.inward(i).wait_send()
+
+        @pl.when(self.at.rim > 0)
+        def _():
+            self.outward(i).wait_send()
+
+        self.deliver(i).wait_send()
+        self.hand(i).wait()
+        self.handn(i).wait()
 
 
 def each(n, body):
@@ -191,27 +193,27 @@
 
 def run_stages(steps, stages):
     def step(u):
-        for lag, stage in stages:
-            h = u - lag
-
-            @pl.when((h >= 0) & (h < KEY_VALUE_HEADS))
+        for lag, pace, count, stage in stages:
+            v = u - lag
+            due = (v >= 0) & (v < count * pace)
+            if pace > 1:
+                due = due & (lax.rem(v, pace) == 0)
+
+            @pl.when(due)
             def _():
-                stage(h)
+                stage(lax.div(v, pace) if pace > 1 else v)
 
     each(steps, step)
 
 
-def main_kernel(groups, count, kv_hbm, q_hbm, docs, counts,
-                o, sib, far, farn, fars, farns, plan,
-                q, kv, mark, marks, given, gathered, bias, vals, exo, exi, inj, injin,
-                ql, kvl, share_s, share_r, mark_s, mark_r, given_s, given_r, info_s, info_r,
-                kv_s, kv_r, flow_s, flow_r):
+def main_kernel(groups, count, kv_hbm, q_hbm, docs_hbm, counts,
+                o, sib, plan,
+                q, kv, docs_in, mark, marks, given, gathered, bias, vals,
+                ql, kvl, docs_s, share_s, share_r, mark_s, mark_r, given_s, given_r, info_s, info_r,
+                kv_s, kv_r):
     at = Place(groups, count)
     me, core, chip, line, group = at.me, at.core, at.chip, at.line, at.group
     chips = count // 2
-    flow = Flow(at, ROUNDS, o, sib, plan, far, farn, fars, farns, exo, exi, inj, injin,
-                flow_s, flow_r, lambda r: r)
-
     def own(h):
         return kv_hbm.at[:, pl.ds(pl.multiple_of(h * KV_COLS, KV_COLS), KV_COLS)]
 
@@ -270,9 +272,10 @@
             body(lax.rem(me + 1 + i, count))
         each(count - 1, one)
 
+    docs = pltpu.make_async_copy(docs_hbm, docs_in, docs_s)
+    docs.start()
     heads(lambda h: local(h).start())
     heads(lambda h: q_copy(h).start())
-    mark[...] = jnp.broadcast_to(docs[...], (8, TILE))
     given[group] = jnp.full((8, TILE), counts[0], jnp.int32)
 
     barrier = pltpu.get_barrier_semaphore()
@@ -280,6 +283,8 @@
     for by in range(1, groups):
         pl.semaphore_signal(barrier, inc=1, device_id={"groups": lax.rem(group + by, groups)},
                             device_id_type=MESH)
+    docs.wait()
+    mark[...] = jnp.broadcast_to(docs_in[...], (8, TILE))
     pl.semaphore_wait(barrier, count - 1 + groups - 1)
 
     has_two_up = chip + 2 < chips
@@ -435,19 +440,12 @@
         attend(h)
         share(h).start()
 
-    def shared(h):
-        @pl.when(h == 0)
-        def _():
-            tally()
-
-        share(h).wait_recv()
-
-    stages = ((0, relay_two), (1, relay_sib), (2, compute), (3, shared)) + flow.stages(3)
-    run_stages(flow.steps(3), stages)
+    run_stages(KEY_VALUE_HEADS + 3, tuple((lag, 1, KEY_VALUE_HEADS, stage) for lag, stage in (
+        (0, relay_two), (2, relay_sib), (3, compute))))
+    tally()
 
     def drain(h):
-        flow.drain(h)
-        share(h).wait_send()
+        share(h).wait()
 
         @pl.when(has_two_up)
         def _():
@@ -479,7 +477,7 @@
             mark_to(k).wait_send()
 
 
-def round_kernel(groups, count, o, sib, plan, turn, far, farn, fars, farns,
+def round_kernel(groups, count, rounds, o, sib, plan, turn, far, farn, fars, farns,
                  exo, exi, inj, injin, flow_s, flow_r):
     at = Place(groups, count)
     barrier = pltpu.get_barrier_semaphore()
@@ -498,51 +496,42 @@
 
     pl.semaphore_wait(barrier, jnp.where(at.rim > 0, 5, 4))
 
-    flow = Flow(at, 1, o, sib, plan, far, farn, fars, farns, exo, exi, inj, injin,
-                flow_s, flow_r, lambda r: turn[0:1, :])
-    run_stages(flow.steps(0), flow.stages(0))
-    heads(flow.drain)
-
-
-def place_kernel(extra, tiles, valid, plan, o, *rest):
-    fars, out, blank, sems = rest[:-3], rest[-3], rest[-2], rest[-1]
+    flow = Flow(at, rounds, SPLITS, o, sib, plan, far, farn, fars, farns, exo, exi, inj, injin,
+                flow_s, flow_r, lambda r: turn[0:1, :] + r)
+    run_stages(flow.steps(0, HOP), flow.stages(0, HOP))
+    each(flow.items, flow.drain)
+
+
+def place_kernel(rounds, tiles, valid, plan, o, far, farn, fars, farns, out, blank, sems):
     me = lax.axis_index("seq")
     core = lax.rem(me, 2)
     slots = out.shape[0] // TILE
     blank[...] = jnp.zeros_like(blank)
-    rank = plan[4 * 8, 0]
-    main, late = fars[:4], fars[4:]
-    turn = jnp.clip(rank, 0, ROUNDS - 1)
-
-    def spot(h, lane, part):
+    turn = jnp.clip(plan[4 * 8, 0], 0, rounds - 1)
+
+    def spot(h, lane, part=0, width=PART_COLS):
         at = (2 * h + lane) * HALF_COLS + part * PART_COLS
-        return pl.ds(pl.multiple_of(at, PART_COLS), PART_COLS)
+        return pl.ds(pl.multiple_of(at, width), width)
 
     def parts(h):
-        mine = [(o.at[h, lane, :, pl.ds(part * PART_COLS, PART_COLS)], spot(h, lane, part))
-                for lane in (0, 1) for part in (0, 1)]
+        mine = [(o.at[h, lane], 0, TILE, spot(h, lane, 0, HALF_COLS)) for lane in (0, 1)]
         where = [spot(h, lane, part) for lane in (core, 1 - core) for part in (0, 1)]
-        theirs = [(ref.at[turn, h], cols) for ref, cols in zip(main, where)]
-        later = [(ref.at[0, h], cols) for ref, cols in zip(late, where)]
-        none = [(blank, cols) for _, cols in mine]
-        return mine, theirs, later, none
+        theirs = [(ref.at[(h * SPLITS + p) * rounds + turn], p * (TILE // SPLITS), TILE // SPLITS, cols)
+                  for ref, cols in zip((far, farn, fars, farns), where) for p in range(SPLITS)]
+        none = [(blank, 0, TILE, pl.ds(pl.multiple_of(h * GROUP_COLS, GROUP_COLS), GROUP_COLS))]
+        return mine, theirs, none
 
     def run(h, c, go):
         for s in range(slots):
             live = s < valid[0]
             own = live & (tiles[0, s] == me)
-            moved = live & jnp.logical_not(own)
-            soon = moved & (rank < ROUNDS) if extra else moved
-            cases = (own, soon, moved & (rank >= ROUNDS), jnp.logical_not(live))
+            cases = (own, live & jnp.logical_not(own), jnp.logical_not(live))
             for case, pieces in zip(cases, parts(h)):
-                if not pieces:
-                    continue
-
                 @pl.when(case)
                 def _():
-                    for k, (src, cols) in enumerate(pieces):
+                    for k, (src, row, rows, cols) in enumerate(pieces):
                         go(pltpu.make_async_copy(
-                            src, out.at[pl.ds(s * TILE, TILE), cols], sems.at[h, s, k]))
+                            src, out.at[pl.ds(s * TILE + row, rows), cols], sems.at[h, s, k]))
         return c
 
     lax.fori_loop(0, KEY_VALUE_HEADS, functools.partial(run, go=lambda x: x.start()), 0)
@@ -554,33 +543,35 @@
     slots = owner_tiles.shape[1]
     H = KEY_VALUE_HEADS
     bf, i32 = jnp.bfloat16, jnp.int32
-    half = (H, TILE, HALF_COLS)
-
-    def part(rounds):
-        return (rounds, H, TILE, PART_COLS)
-
-    *held, plan = pl.pallas_call(
+
+    def stay(x):
+        return pltpu.with_memory_space_constraint(x, pltpu.HBM)
+
+    def near(x):
+        return pltpu.with_memory_space_constraint(x, pltpu.VMEM)
+
+    o, sib, plan = pl.pallas_call(
         functools.partial(main_kernel, groups, count),
         out_shape=[
-            jax.ShapeDtypeStruct((H, 2, TILE, HALF_COLS), bf),
-            jax.ShapeDtypeStruct(half, bf),
-        ] + [jax.ShapeDtypeStruct(part(ROUNDS), bf)] * 4 + [
-            jax.ShapeDtypeStruct((48, TILE), i32),
+            pltpu.VMEM((H, 2, TILE, HALF_COLS), bf),
+            pltpu.VMEM((H, TILE, HALF_COLS), bf),
+            pltpu.VMEM((48, TILE), i32),
         ],
-        in_specs=[HBM, HBM, VMEM, SMEM],
-        out_specs=[VMEM] * 7,
+        in_specs=[HBM, HBM, HBM, SMEM],
+        out_specs=[VMEM] * 3,
         scratch_shapes=[
             pltpu.VMEM(queries.shape, bf),
             pltpu.VMEM((H, 6, TILE, KV_COLS), bf),
+            pltpu.VMEM((1, TILE), i32),
             pltpu.VMEM((8, TILE), i32),
             pltpu.VMEM((BACK, 8, TILE), i32),
             pltpu.VMEM((groups, 8, TILE), i32),
             pltpu.VMEM((count, groups, 8, TILE), i32),
             pltpu.VMEM((TILE, NEAR_TILES * TILE), jnp.float32),
             pltpu.VMEM((NEAR_TILES * TILE, 2 * HEAD_WIDTH), bf),
-        ] + [pltpu.VMEM(part(ROUNDS), bf)] * 4 + [
             DMA((H,)),
             DMA((H,)),
+            DMA(()),
             DMA((H,)),
             DMA((H,)),
             DMA((BACK,)),
@@ -591,46 +582,49 @@
             DMA((count,)),
             DMA((5, H)),
             DMA((H, 6)),
-            DMA((6, ROUNDS, H)),
-            DMA((6, ROUNDS, H)),
         ],
         compiler_params=pltpu.CompilerParams(
-            collective_id=0, has_side_effects=True, vmem_limit_bytes=40 << 20),
-    )(keyvalue, queries, doc_ids[None, :], tile_counts)
-    o, sib, *far = held
-
-    def again(turn):
-        turns = jnp.full((8, TILE), turn, i32)
+            collective_id=0, has_side_effects=True, vmem_limit_bytes=16 << 20),
+    )(stay(keyvalue), stay(queries), stay(doc_ids[None, :]), tile_counts)
+
+    def rounds_from(turn, rounds, number):
+        items = H * SPLITS * rounds
+        part = pltpu.VMEM((items, TILE // SPLITS, PART_COLS), bf)
         return pl.pallas_call(
-            functools.partial(round_kernel, groups, count),
-            out_shape=[jax.ShapeDtypeStruct(part(1), bf)] * 4,
+            functools.partial(round_kernel, groups, count, rounds),
+            out_shape=[part] * 4,
             in_specs=[VMEM] * 4,
             out_specs=[VMEM] * 4,
-            scratch_shapes=[pltpu.VMEM(part(1), bf)] * 4 + [DMA((6, 1, H)), DMA((6, 1, H))],
+            scratch_shapes=[part] * 4 + [DMA((6, items))] * 2,
             compiler_params=pltpu.CompilerParams(
-                collective_id=1, has_side_effects=True, vmem_limit_bytes=24 << 20),
-        )(o, sib, plan, turns)
-
-    def place(late):
+                collective_id=number, has_side_effects=True, vmem_limit_bytes=(8 + 4 * rounds) << 20),
+        )(near(o), near(sib), near(plan), jnp.full((8, TILE), turn, i32))
+
+    def place(rounds, far):
         return pl.pallas_call(
-            functools.partial(place_kernel, bool(late)),
-            out_shape=jax.ShapeDtypeStruct((slots * TILE, width), bf),
-            in_specs=[SMEM] * 3 + [VMEM] * (5 + len(late)),
+            functools.partial(place_kernel, rounds),
+            out_shape=pltpu.HBM((slots * TILE, width), bf),
+            in_specs=[SMEM] * 3 + [VMEM] * 5,
             out_specs=pl.BlockSpec(memory_space=pl.ANY),
-            scratch_shapes=[pltpu.VMEM((TILE, PART_COLS), bf), DMA((H, slots, 4))],
-            compiler_params=pltpu.CompilerParams(vmem_limit_bytes=16 << 20),
-        )(owner_tiles, tile_counts, plan, o, *far, *late)
+            scratch_shapes=[pltpu.VMEM((TILE, GROUP_COLS), bf), DMA((H, slots, 4 * SPLITS))],
+            compiler_params=pltpu.CompilerParams(vmem_limit_bytes=8 << 20),
+        )(owner_tiles, tile_counts, plan, near(o), *map(near, far))
 
     most = plan[40, 0]
 
-    def more():
-        def one(turn, kept):
+    def fused(rounds):
+        return lambda: place(rounds, rounds_from(0, rounds, rounds))
+
+    def one_by_one():
+        def again(turn, kept):
             here = plan[32, 0] == turn
-            return tuple(jnp.where(here, n, k) for n, k in zip(again(turn), kept))
-
-        return place(lax.fori_loop(ROUNDS, most, one, tuple(jnp.zeros(part(1), bf) for _ in range(4))))
-
-    return lax.cond(most > ROUNDS, more, lambda: place(()))
+            return tuple(jnp.where(here, n, k) for n, k in zip(rounds_from(turn, 1, FUSED + 1), kept))
+
+        empty = jnp.zeros((H * SPLITS, TILE // SPLITS, PART_COLS), bf)
+        return place(1, lax.fori_loop(0, most, again, (empty,) * 4))
+
+    return lax.switch(jnp.minimum(most, FUSED + 1) - 1,
+                      [fused(r) for r in range(1, FUSED + 1)] + [one_by_one])
 
 
 def solution(mesh):

time: 87.8 us -> 92.7 us (1.056)
  Pallas kernels: 80.4 us -> 90.5 us
  local copies, waits for them, and re-layouts: 5.82 us -> 0.58 us
    pallas_call x1 -> x2, Pallas kernels: 4.49 us -> 65.9 us  [the longest x1 61.7 us: rounds_from(): pl.pallas_call(functools.partial(round_kernel, groups, count, rounds), ou...]
    pallas_call x1, Pallas kernels: 75.9 us -> 24.7 us  [local(): pl.pallas_call(functools.partial(main_kernel, groups, count), out_shape=[...]
    unnamed x8 -> x2, local copies, waits for them, and re-layouts: 5.29 us -> 0.01 us
where the time goes in v1:
time: 92.7 us; the launch traced here: 92.5 us
  Pallas kernels  90.5 us (98%)
  between operations  1.36 us (1%)
    pallas_call x1, Pallas kernels, rounds_from(): pl.pallas_call(functools.partial(round_kernel, groups, count, rounds), ou...  61.7 us
    pallas_call x1, Pallas kernels, local(): pl.pallas_call(functools.partial(main_kernel, groups, count), out_shape=[...  24.7 us
    pallas_call x1, Pallas kernels, place(): pl.pallas_call(functools.partial(place_kernel, rounds), out_shape=pltpu.H...  4.17 us

profile of v1, /device:TPU:0, one launch (start us, length us, event | category | flops | bytes accessed | tf_op | source)
XLA Modules:
  0.0 92.5 jit_solution(68517396834986610)
XLA Ops:
  0.0 0.0 copy-start.12
  0.7 24.7 %shard_map.60 = (bf16[8,2,128,512]{3,2,1,0:T(8,128)(2,1)S(1)}, bf16[8,128,512]{2,1,0:T(8,128)(2,1)S(1)}, s32[48,128]{1,0:T(8,128)S(1)}) custom-call(bf16[128,2048]{1,0:T(8,128)(2,1)} %kv_hbm.1, bf16[128,8192]{1,0:T(8,128)(2,1)} %q_hbm.1, s32[1,128]{1,0:T(1,128)} %bitcast.5, s32[1]{0:T(128)S(6)} %copy.32.counts), custom_call_target="tpu_custom_call" | custom-call | tf_op jit(solution)/shard_map/pallas_call | solution.py:553
  25.3 0.6 slice.6
  26.6 0.0 copy-done.12
  26.6 65.9 %conditional.1 = (bf16[256,8192]{1,0:T(8,128)(2,1)}) conditional(s32[]{:T(128)} %clamp.3, (bf16[8,2,128,512]{3,2,1,0:T(8,128)(2,1)S(1)}, bf16[8,128,512]{2,1,0:T(8,128)(2,1)S(1)}, s32[48,128]{1,0:T(8,128)S(1)}, s32[1,2]{1,0:T(1,128)S(1)}, s32[1]{0:T(128)}) %tuple.53, (bf16[8,2,128,512]{3,2,1,0:T(8,128)(2,1)S(1)}, ...), branch_computations={%region_0.0_spmd, %region_1.0_spmd, %region_2.0_spmd, %region_3.0_... | conditional | flops 1048579 | bytes 33559100 | solution.py:626
  26.6 61.7 %branch_2_fun.2 = (bf16[24,128,256]{2,1,0:T(8,128)(2,1)S(1)}, bf16[24,128,256]{2,1,0:T(8,128)(2,1)S(1)}, bf16[24,128,256]{2,1,0:T(8,128)(2,1)S(1)}, bf16[24,128,256]{2,1,0:T(8,128)(2,1)S(1)}) custom-call(bf16[8,2,128,512]{3,2,1,0:T(8,128)(2,1)S(1)} %get-tuple-element.120.o, bf16[8,128,512]{2,1,0:T(8,128)(2,1)S(1)} %get-tuple-element.121.sib, ...), custom_call_target="tpu_custom_call" | custom-call | tf_op jit(solution)/shard_map/cond/branch_2_fun/pallas_call | solution.py:593
  88.4 4.2 %branch_2_fun.3 = bf16[256,8192]{1,0:T(8,128)(2,1)} custom-call(s32[1,2]{1,0:T(1,128)S(1)} %get-tuple-element.117.tiles, s32[1]{0:T(128)} %get-tuple-element.118.valid, s32[48,128]{1,0:T(8,128)S(1)} %get-tuple-element.119.plan, bf16[8,2,128,512]{3,2,1,0:T(8,128)(2,1)S(1)} %get-tuple-element.120.o, bf16[24,128,256]{2,1,0:T(8,128)(2,1)S(1)} %get-tuple-element.122.far, ...), custom_call_target="tpu_custom_call" | custom-call | tf_op jit(solution)/shard_map/cond/branch_2_fun/pallas_call | solution.py:604
  (1 shorter events, 0.0 us)
Async XLA Ops:
  0.0 26.6 %copy-start.12 = (s32[1,2]{1,0:T(1,128)S(1)}, s32[1,2]{1,0:T(1,128)}, u32[]{:S(2)}) copy-start(s32[1,2]{1,0:T(1,128)} %param.15) | copy-start | bytes 28
